TPU v7x, 256 devices: a whole 4x4x8 slice. The times are simulated.
256 devices in a mesh: seq: 64 (over z, y, core), ch: 4 (over x).
Axes of the slice: x: 4, y: 4, z: 8, core: 2. Of those that a mesh axis runs over, the one named last changes fastest.
Arguments:
- signal: bfloat16 [32768, 1024], P('seq', 'ch'), may hold values from -6 to 6
- gate_values: bfloat16 [32768, 1024], P('seq', 'ch'), may hold values from -6 to 6
- cotangent: bfloat16 [32768, 1024], P('seq', 'ch'), may hold values from -6 to 6
- skip_gain: float32 [1024], P('ch'), may hold values from -3 to 3
- log_rate: float32 [1024], P('ch'), as said below
- embed_weight: float32 [33, 64], replicated, may hold values from -1 to 1
- sine_freq: float32 [64], replicated, may hold values from 1 to 8
- mid_weight: float32 [64, 64], replicated, may hold values from -0.75 to 0.75
- out_weight: float32 [64, 1024], P(None, 'ch'), may hold values from -0.75 to 0.75
Outputs:
- output: bfloat16 [32768, 1024], P('seq', 'ch')
- signal_grad: bfloat16 [32768, 1024], P('seq', 'ch')
- gate_grad: bfloat16 [32768, 1024], P('seq', 'ch')
- skip_grad: float32 [1024], P('ch')
- rate_grad: float32 [1024], P('ch')
- out_weight_grad: float32 [64, 1024], P(None, 'ch')
- embed_grad: float32 [33, 64], replicated
- mid_grad: float32 [64, 64], replicated
- freq_grad: float32 [64], replicated
Inputs may be any that keep to these rules, and one draw needn't show every extreme that they name: exp(log_rate) lies between 0.25 / 32768 and 1 / 30.
All inputs are finite; a program needn't handle non-finite values.
Results may differ from a plain program's by a relative error of at most 0.0051.
Values may be sent and summed in bfloat16 or wider, within the bound.
A program may use at most 128 MiB of HBM per device.

v0:
```python
from functools import partial
import math
import jax
import jax.numpy as jnp
from jax import lax
from jax.sharding import PartitionSpec as P

highest = lax.Precision.HIGHEST
phase_modulus = 4093
band_stride = 255


def unit_angle(product, modulus):
    return (product % modulus).astype(jnp.float32) * (2.0 * math.pi / modulus)


def position_features(positions, seq_total, band_count):
    band_steps = 1 + band_stride * jnp.arange(band_count, dtype=jnp.int32)
    angles = unit_angle(positions[:, None] * band_steps[None, :], phase_modulus)
    position_ramp = positions.astype(jnp.float32)[:, None] / seq_total
    return jnp.concatenate([position_ramp, jnp.cos(angles), jnp.sin(angles)], axis=1)


def lower_layers(features, embed_weight, sine_freq, mid_weight):
    first_pre = jnp.dot(
        features, embed_weight, precision=highest, preferred_element_type=jnp.float32
    )
    first_act = jnp.sin(sine_freq[None, :] * first_pre)
    second_pre = jnp.dot(
        first_act, mid_weight, precision=highest, preferred_element_type=jnp.float32
    )
    return jnp.sin(sine_freq[None, :] * second_pre)


def split_length(length):
    leading = 1
    for candidate in range(1, math.isqrt(length) + 1):
        if length % candidate == 0:
            leading = candidate
    return (leading, length // leading)


def dft_tables(size_left, size_right, modulus):
    left_index = jnp.arange(size_left, dtype=jnp.int32)
    right_index = jnp.arange(size_right, dtype=jnp.int32)
    angles = unit_angle(left_index[:, None] * right_index[None, :], modulus)
    return (jnp.cos(angles), jnp.sin(angles))


def einsum_high(pattern, matrix, values):
    return jnp.einsum(pattern, matrix, values, precision=highest)


def local_forward(real_part, imag_part):
    stacks, length, channels = real_part.shape
    leading, trailing = split_length(length)
    real_part = real_part.reshape(stacks, leading, trailing, channels)
    imag_part = imag_part.reshape(stacks, leading, trailing, channels)
    cos_lead, sin_lead = dft_tables(leading, leading, leading)
    step_real = einsum_high("ka,eabc->ekbc", cos_lead, real_part) + einsum_high(
        "ka,eabc->ekbc", sin_lead, imag_part
    )
    step_imag = einsum_high("ka,eabc->ekbc", cos_lead, imag_part) - einsum_high(
        "ka,eabc->ekbc", sin_lead, real_part
    )
    cos_mid, sin_mid = dft_tables(leading, trailing, length)
    cos_mid = cos_mid[None, :, :, None]
    sin_mid = sin_mid[None, :, :, None]
    turned_real = step_real * cos_mid + step_imag * sin_mid
    turned_imag = step_imag * cos_mid - step_real * sin_mid
    cos_tail, sin_tail = dft_tables(trailing, trailing, trailing)
    out_real = einsum_high("qb,ekbc->ekqc", cos_tail, turned_real) + einsum_high(
        "qb,ekbc->ekqc", sin_tail, turned_imag
    )
    out_imag = einsum_high("qb,ekbc->ekqc", cos_tail, turned_imag) - einsum_high(
        "qb,ekbc->ekqc", sin_tail, turned_real
    )
    return (out_real, out_imag)


def local_inverse(real_part, imag_part):
    stacks, leading, trailing, channels = real_part.shape
    length = leading * trailing
    cos_tail, sin_tail = dft_tables(trailing, trailing, trailing)
    step_real = einsum_high("bq,ekqc->ekbc", cos_tail, real_part) - einsum_high(
        "bq,ekqc->ekbc", sin_tail, imag_part
    )
    step_imag = einsum_high("bq,ekqc->ekbc", cos_tail, imag_part) + einsum_high(
        "bq,ekqc->ekbc", sin_tail, real_part
    )
    cos_mid, sin_mid = dft_tables(leading, trailing, length)
    cos_mid = cos_mid[None, :, :, None]
    sin_mid = sin_mid[None, :, :, None]
    turned_real = step_real * cos_mid - step_imag * sin_mid
    turned_imag = step_imag * cos_mid + step_real * sin_mid
    cos_lead, sin_lead = dft_tables(leading, leading, leading)
    out_real = einsum_high("ak,ekbc->eabc", cos_lead, turned_real) - einsum_high(
        "ak,ekbc->eabc", sin_lead, turned_imag
    )
    out_imag = einsum_high("ak,ekbc->eabc", cos_lead, turned_imag) + einsum_high(
        "ak,ekbc->eabc", sin_lead, turned_real
    )
    return (out_real.reshape(stacks, length, channels), out_imag.reshape(stacks, length, channels))


def section_tables(devices, fft_length):
    sources = jnp.arange(devices, dtype=jnp.int32)
    row_index = jnp.arange(2 * devices, dtype=jnp.int32)
    fwd_angles = unit_angle(row_index[:, None] * sources[None, :], 2 * devices)
    inv_angles = unit_angle(sources[:, None] * row_index[None, :], 2 * devices)
    cos_fwd = jnp.cos(fwd_angles)
    sin_fwd = -jnp.sin(fwd_angles)
    cos_inv = jnp.cos(inv_angles) / fft_length
    sin_inv = -jnp.sin(inv_angles) / fft_length
    return (cos_fwd, sin_fwd, cos_inv, sin_inv)


def on_device(
    signal,
    gate_values,
    cotangent,
    skip_gain,
    log_rate,
    embed_weight,
    sine_freq,
    mid_weight,
    out_weight,
):
    devices = lax.axis_size("seq")
    seq_index = lax.axis_index("seq")
    local_len, channels = signal.shape
    seq_total = devices * local_len
    fft_length = 2 * seq_total
    cos_fwd, sin_fwd, cos_inv, sin_inv = section_tables(devices, fft_length)
    column_index = jnp.arange(local_len, dtype=jnp.int32)
    positions = seq_index * local_len + column_index

    def section_forward(pieces):
        pieces = pieces.astype(jnp.float32)
        return (
            einsum_high("rs,sjc->rjc", cos_fwd, pieces),
            einsum_high("rs,sjc->rjc", sin_fwd, pieces),
        )

    def row_frequencies():
        return 2 * seq_index + jnp.arange(2, dtype=jnp.int32)

    def expand_rows(received):
        real_part, imag_part = received
        angles = unit_angle(row_frequencies()[:, None] * column_index[None, :], fft_length)[
            :, :, None
        ]
        cos_rows = jnp.cos(angles)
        sin_rows = jnp.sin(angles)
        rows_real = real_part * cos_rows + imag_part * sin_rows
        rows_imag = imag_part * cos_rows - real_part * sin_rows
        return local_forward(rows_real, rows_imag)

    def to_spectrum(columns):
        return expand_rows(
            (
                lax.all_to_all(columns[0], "seq", split_axis=0, concat_axis=1, tiled=True),
                lax.all_to_all(columns[1], "seq", split_axis=0, concat_axis=1, tiled=True),
            )
        )

    def section_inverse(received):
        real_part, imag_part = received
        return einsum_high("br,rjc->bjc", cos_inv, real_part) + einsum_high(
            "br,rjc->bjc", sin_inv, imag_part
        )

    def to_positions(spectrum):
        real_part, imag_part = local_inverse(spectrum[0], spectrum[1])
        angles = unit_angle(row_frequencies()[:, None] * column_index[None, :], fft_length)[
            :, :, None
        ]
        cos_rows = jnp.cos(angles)
        sin_rows = jnp.sin(angles)
        plain_real = real_part * cos_rows - imag_part * sin_rows
        plain_imag = imag_part * cos_rows + real_part * sin_rows
        packed = (plain_real, plain_imag)
        rows_back = section_inverse(
            (
                lax.all_to_all(packed[0], "seq", split_axis=1, concat_axis=0, tiled=True),
                lax.all_to_all(packed[1], "seq", split_axis=1, concat_axis=0, tiled=True),
            )
        )
        field = lax.all_to_all(rows_back, "seq", split_axis=0, concat_axis=1, tiled=True)
        return field[0]

    band_count = (embed_weight.shape[0] - 1) // 2
    features = position_features(positions, seq_total, band_count)
    upper_act, lower_pull = jax.vjp(
        partial(lower_layers, features), embed_weight, sine_freq, mid_weight
    )
    raw_filter = jnp.dot(
        upper_act, out_weight, precision=highest, preferred_element_type=jnp.float32
    )
    decay_rate = jnp.exp(log_rate)
    place = positions.astype(jnp.float32)[:, None]
    envelope = jnp.exp(-decay_rate[None, :] * place) * jnp.sqrt(2.0 * decay_rate)[None, :]
    signal_f = signal.astype(jnp.float32)
    gate_f = gate_values.astype(jnp.float32)
    cot_f = cotangent.astype(jnp.float32)
    upstream_bf = (cot_f * gate_f).astype(jnp.bfloat16)
    upstream = lax.optimization_barrier(upstream_bf).astype(jnp.float32)
    signal_cols = section_forward(
        lax.all_to_all(signal[None], "seq", split_axis=1, concat_axis=0, tiled=True)
    )
    kernel = raw_filter * envelope
    kernel_cols = section_forward(
        lax.all_to_all(kernel[None], "seq", split_axis=1, concat_axis=0, tiled=True)
    )
    signal_spec = to_spectrum(signal_cols)
    kernel_spec = to_spectrum(kernel_cols)
    conv_spec = (
        kernel_spec[0] * signal_spec[0] - kernel_spec[1] * signal_spec[1],
        kernel_spec[0] * signal_spec[1] + kernel_spec[1] * signal_spec[0],
    )
    conv_out = to_positions(conv_spec)
    upstream_cols = section_forward(
        lax.all_to_all(upstream_bf[None], "seq", split_axis=1, concat_axis=0, tiled=True)
    )
    upstream_spec = to_spectrum(upstream_cols)
    joined_real = jnp.concatenate(
        [
            kernel_spec[0] * upstream_spec[0] + kernel_spec[1] * upstream_spec[1],
            signal_spec[0] * upstream_spec[0] + signal_spec[1] * upstream_spec[1],
        ],
        axis=3,
    )
    joined_imag = jnp.concatenate(
        [
            kernel_spec[0] * upstream_spec[1] - kernel_spec[1] * upstream_spec[0],
            signal_spec[0] * upstream_spec[1] - signal_spec[1] * upstream_spec[0],
        ],
        axis=3,
    )
    back_fields = to_positions((joined_real, joined_imag))
    signal_corr = back_fields[:, :channels]
    kernel_grad = back_fields[:, channels:]
    mixed_sum = conv_out + skip_gain[None, :] * signal_f
    output = (gate_f * mixed_sum).astype(jnp.bfloat16)
    gate_grad = (cot_f * mixed_sum).astype(jnp.bfloat16)
    signal_grad = (skip_gain[None, :] * upstream + signal_corr).astype(jnp.bfloat16)
    skip_part = jnp.sum(upstream * signal_f, axis=0)
    rate_part = jnp.sum(
        kernel_grad * raw_filter * envelope * (0.5 - decay_rate[None, :] * place), axis=0
    )
    scaled_kernel = kernel_grad * envelope
    out_part = jnp.dot(
        upper_act.T, scaled_kernel, precision=highest, preferred_element_type=jnp.float32
    )
    upper_grad = jnp.dot(
        scaled_kernel, out_weight.T, precision=highest, preferred_element_type=jnp.float32
    )
    upper_grad = lax.psum(upper_grad, "ch")
    embed_part, freq_part, mid_part = lower_pull(upper_grad)
    out_sum, skip_sum, rate_sum, embed_sum, mid_sum, freq_sum = lax.psum(
        (out_part, skip_part, rate_part, embed_part, mid_part, freq_part), "seq"
    )
    grad_scale = 1.0 / math.sqrt(seq_total)
    return (
        output,
        signal_grad,
        gate_grad,
        skip_sum * grad_scale,
        rate_sum * grad_scale,
        out_sum * grad_scale,
        embed_sum * grad_scale,
        mid_sum * grad_scale,
        freq_sum * grad_scale,
    )


def solution(mesh):
    in_specs = (
        P("seq", "ch"),
        P("seq", "ch"),
        P("seq", "ch"),
        P("ch"),
        P("ch"),
        P(),
        P(),
        P(),
        P(None, "ch"),
    )
    out_specs = (
        P("seq", "ch"),
        P("seq", "ch"),
        P("seq", "ch"),
        P("ch"),
        P("ch"),
        P(None, "ch"),
        P(),
        P(),
        P(),
    )
    return jax.shard_map(
        on_device, mesh=mesh, in_specs=in_specs, out_specs=out_specs, check_vma=False
    )
```

profile of v0, /device:TPU:4, one launch (start us, length us, event | category | flops | bytes accessed | tf_op | source)
XLA Modules:
  0.0 1065.5 jit_solution(7820798269313045726)
XLA Ops:
  9.3 2.2 reduce
  12.3 12.1 %all-to-all-start.9 = ((bf16[64,2,1024]{2,1,0:T(2,128)(2,1)}), bf16[64,2,1024]{2,1,0:T(2,128)(2,1)S(1)}, u32[]{:S(2)}, u32[]{:S(2)}) async-start(bf16[64,2,1024]{2,1,0:T(2,128)(2,1)} %reshape.243), calls=%async_computation.9 | async-start | bytes 524288 | tf_op jit(solution)/shard_map/all_to_all | solution.py:223
  24.9 2.2 reduce.1
  29.3 8.1 all-to-all-done.9
  37.4 4.9 all-to-all-start.3
  45.5 9.8 all-to-all-done.3
  55.3 4.9 all-to-all-start
  62.9 15.0 %all-to-all-done = f32[1,512,256]{2,0,1:T(1,128)S(1)} async-done(((f32[1,512,256]{2,0,1:T(1,128)}), f32[1,512,256]{2,0,1:T(1,128)S(1)}, u32[]{:S(2)}, u32[]{:S(2)}) %all-to-all-start) | async-done | bytes 524320 | tf_op jit(solution)/shard_map/all_to_all | solution.py:213
  78.7 6.0 all-to-all-start.11
  87.1 26.5 %all-to-all-done.11 = f32[128,8,256]{2,1,0:T(8,128)S(1)} async-done(((f32[128,8,256]{2,1,0:T(8,128)}), f32[128,8,256]{2,1,0:T(8,128)S(1)}, u32[]{:S(2)}, u32[]{:S(2)}) %all-to-all-start.11) | async-done | bytes 1048608 | tf_op jit(solution)/shard_map/all_to_all | solution.py:163
  113.6 5.6 all-to-all-start.10
  123.6 24.5 %all-to-all-done.10 = f32[128,8,256]{2,1,0:T(8,128)S(1)} async-done(((f32[128,8,256]{2,1,0:T(8,128)}), f32[128,8,256]{2,1,0:T(8,128)S(1)}, u32[]{:S(2)}, u32[]{:S(2)}) %all-to-all-start.10) | async-done | bytes 1048608 | tf_op jit(solution)/shard_map/all_to_all | solution.py:162
  148.1 5.8 all-to-all-start.5
  156.2 26.4 %all-to-all-done.5 = f32[128,8,256]{2,1,0:T(8,128)} async-done(((f32[128,8,256]{2,1,0:T(8,128)}), f32[128,8,256]{2,1,0:T(8,128)}, u32[]{:S(2)}, u32[]{:S(2)}) %all-to-all-start.5) | async-done | bytes 1048608 | tf_op jit(solution)/shard_map/all_to_all | solution.py:163
  182.6 6.0 all-to-all-start.4
  191.4 25.9 %all-to-all-done.4 = f32[128,8,256]{2,1,0:T(8,128)} async-done(((f32[128,8,256]{2,1,0:T(8,128)}), f32[128,8,256]{2,1,0:T(8,128)}, u32[]{:S(2)}, u32[]{:S(2)}) %all-to-all-start.4) | async-done | bytes 1048608 | tf_op jit(solution)/shard_map/all_to_all | solution.py:162
  217.3 5.8 all-to-all-start.2
  226.0 25.9 %all-to-all-done.2 = f32[128,8,256]{2,1,0:T(8,128)} async-done(((f32[128,8,256]{2,1,0:T(8,128)}), f32[128,8,256]{2,1,0:T(8,128)}, u32[]{:S(2)}, u32[]{:S(2)}) %all-to-all-start.2) | async-done | bytes 1048608 | tf_op jit(solution)/shard_map/all_to_all | solution.py:163
  251.9 14.6 %all-to-all-start.1 = ((f32[128,8,256]{2,1,0:T(8,128)}), f32[128,8,256]{2,1,0:T(8,128)}, u32[]{:S(2)}, u32[]{:S(2)}) async-start(f32[128,8,256]{2,1,0:T(8,128)} %copy.247), calls=%async_computation.1 | async-start | bytes 2097152 | tf_op jit(solution)/shard_map/all_to_all | solution.py:162
  268.4 2.3 copy.266
  270.7 2.3 copy.263
  273.0 2.3 copy.251
  275.3 11.2 %all-to-all-done.1 = f32[128,8,256]{2,1,0:T(8,128)} async-done(((f32[128,8,256]{2,1,0:T(8,128)}), f32[128,8,256]{2,1,0:T(8,128)}, u32[]{:S(2)}, u32[]{:S(2)}) %all-to-all-start.1) | async-done | bytes 1048608 | tf_op jit(solution)/shard_map/all_to_all | solution.py:162
  288.3 2.1 fusion.28
  308.6 2.4 multiply_subtract_fusion
  312.7 2.1 fusion.60
  330.4 2.4 add_bitcast_fusion.3
  332.8 3.4 fusion.10
  336.2 3.5 fusion.11
  354.0 2.0 copy.283
  356.0 5.8 all-to-all-start.6
  361.8 4.0 fusion.14
  365.9 3.0 subtract_bitcast_fusion.1
  368.8 3.2 fusion.4
  372.0 3.4 subtract_bitcast_fusion
  377.1 3.2 fusion.2
  380.3 3.4 add_bitcast_fusion
  385.5 3.0 copy.311
  388.4 2.1 all-to-all-done.6
  390.5 8.5 all-to-all-start.12
  399.1 3.0 copy.314
  402.0 48.2 %all-to-all-done.12 = f32[2,512,512]{2,0,1:T(2,128)} async-done(((f32[2,512,512]{2,0,1:T(2,128)}), f32[2,512,512]{2,0,1:T(2,128)}, u32[]{:S(2)}, u32[]{:S(2)}) %all-to-all-start.12) | async-done | bytes 2097184 | tf_op jit(solution)/shard_map/all_to_all | solution.py:185
  450.3 5.3 all-to-all-start.13
  455.6 3.0 copy.286
  458.6 48.4 %all-to-all-done.13 = f32[2,512,512]{2,0,1:T(2,128)S(1)} async-done(((f32[2,512,512]{2,0,1:T(2,128)}), f32[2,512,512]{2,0,1:T(2,128)S(1)}, u32[]{:S(2)}, u32[]{:S(2)}) %all-to-all-start.13) | async-done | bytes 2097184 | tf_op jit(solution)/shard_map/all_to_all | solution.py:186
  507.0 5.6 all-to-all-start.7
  512.6 2.0 copy.419
  514.6 3.0 copy.313
  517.5 3.7 all_to_all.213
  521.6 3.0 copy.316
  524.6 3.8 all_to_all.217
  532.9 8.4 all-to-all-done.7
  541.3 6.0 all-to-all-start.14
  558.0 18.0 %all-to-all-done.14 = f32[64,8,512]{2,1,0:T(8,128)} async-done(((f32[64,8,512]{2,1,0:T(8,128)}), f32[64,8,512]{2,1,0:T(8,128)}, u32[]{:S(2)}, u32[]{:S(2)}) %all-to-all-start.14) | async-done | bytes 1048608 | tf_op jit(solution)/shard_map/all_to_all | solution.py:189
  576.1 5.6 all-to-all-start.8
  581.7 2.6 fusion.98
  584.4 2.5 fusion.96
  586.9 12.4 %all-to-all-done.8 = f32[64,8,256]{2,1,0:T(8,128)S(1)} async-done(((f32[64,8,256]{2,1,0:T(8,128)}), f32[64,8,256]{2,1,0:T(8,128)S(1)}, u32[]{:S(2)}, u32[]{:S(2)}) %all-to-all-start.8) | async-done | bytes 524320 | tf_op jit(solution)/shard_map/all_to_all | solution.py:189
  599.3 2.5 multiply_reduce_fusion
  601.9 153.4 %all-reduce.4.cloned.1.call-done = f32[64,256]{1,0:T(8,128)} async-done(((f32[64,256]{1,0:T(8,128)}), f32[64,256]{1,0:T(8,128)}) %all-reduce.4.cloned.1.call-update) | async-done | bytes 65552 | tf_op jit(solution)/shard_map/psum | solution.py:260
  756.7 43.4 %all-reduce.6.cloned.1.call-done = f32[512,64]{0,1:T(8,128)} async-done(((f32[512,64]{0,1:T(8,128)}), f32[512,64]{0,1:T(8,128)}) %all-reduce.6.cloned.1.call-update) | async-done | bytes 131088 | tf_op jit(solution)/shard_map/psum | solution.py:258
  800.1 2.1 multiply_reduce_fusion.1
  804.1 2.1 fusion.116
  806.2 249.2 %all-reduce = (f32[256]{0:T(256)S(1)}, f32[256]{0:T(256)S(1)}, f32[33,64]{1,0:T(8,128)S(1)}, f32[64,64]{1,0:T(8,128)S(1)}, f32[64]{0:T(128)S(1)}) all-reduce(f32[256]{0:T(256)S(1)} %get-tuple-element.48, f32[256]{0:T(256)S(1)} %get-tuple-element.44, f32[33,64]{1,0:T(8,128)S(1)} %fusion.114, ...), channel_id=1, replica_groups=mesh['seq'=64,'ch'=4] {'seq'}, use_global_device_ids=true, to_apply=%region_1.2 | all-reduce | flops 6784 | bytes 54272 | tf_op jit(solution)/shard_map/psum | solution.py:260
  (152 shorter events, 105.2 us)
Async XLA Ops:
  7.2 35.7 %copy-start = (f32[64,256]{1,0:T(8,128)S(1)}, f32[64,256]{1,0:T(8,128)}, u32[]{:S(2)}) copy-start(f32[64,256]{1,0:T(8,128)} %param.17) | copy-start | bytes 196612
  7.2 17.3 %copy-start.13 = (bf16[512,256]{1,0:T(8,128)(2,1)S(1)}, bf16[512,256]{1,0:T(8,128)(2,1)}, u32[]{:S(2)}) copy-start(bf16[512,256]{1,0:T(8,128)(2,1)} %param.9) | copy-start | bytes 786436
  8.8 19.4 %copy-start.18 = (f32[33,64]{1,0:T(8,128)S(1)}, f32[33,64]{1,0:T(8,128)}, u32[]{:S(2)}) copy-start(f32[33,64]{1,0:T(8,128)} %param.14) | copy-start | bytes 25348
  9.3 19.2 %copy-start.15 = (f32[64,64]{1,0:T(8,128)S(1)}, f32[64,64]{1,0:T(8,128)}, u32[]{:S(2)}) copy-start(f32[64,64]{1,0:T(8,128)} %param.16) | copy-start | bytes 49156
  9.3 19.2 %copy-start.17 = (f32[64]{0:T(128)S(1)}, f32[64]{0:T(128)}, u32[]{:S(2)}) copy-start(f32[64]{0:T(128)} %param.15) | copy-start | bytes 772
  11.5 30.8 %copy-start.22 = (f32[256]{0:T(256)S(1)}, f32[256]{0:T(256)}, u32[]{:S(2)}) copy-start(f32[256]{0:T(256)} %param.13) | copy-start | bytes 3076
  12.3 25.1 %all-to-all-start.9 = ((bf16[64,2,1024]{2,1,0:T(2,128)(2,1)}), bf16[64,2,1024]{2,1,0:T(2,128)(2,1)S(1)}, u32[]{:S(2)}, u32[]{:S(2)}) async-start(bf16[64,2,1024]{2,1,0:T(2,128)(2,1)} %reshape.243), calls=%async_computation.9 | async-start | bytes 524288 | tf_op jit(solution)/shard_map/all_to_all | solution.py:223
  37.4 17.9 %all-to-all-start.3 = ((bf16[64,2,1024]{2,1,0:T(2,128)(2,1)}), bf16[64,2,1024]{2,1,0:T(2,128)(2,1)S(1)}, u32[]{:S(2)}, u32[]{:S(2)}) async-start(bf16[64,2,1024]{2,1,0:T(2,128)(2,1)} %reshape.241), calls=%async_computation.3 | async-start | bytes 524288 | tf_op jit(solution)/shard_map/all_to_all | solution.py:209
  42.9 12.4 %copy-start.19 = (f32[256]{0:T(256)}, f32[256]{0:T(256)S(1)}, u32[]{:S(2)}) copy-start(f32[256]{0:T(256)S(1)} %get-tuple-element.65) | copy-start | bytes 3076
  55.3 5.2 copy-start.9
  55.3 22.6 %all-to-all-start = ((f32[1,512,256]{2,0,1:T(1,128)}), f32[1,512,256]{2,0,1:T(1,128)S(1)}, u32[]{:S(2)}, u32[]{:S(2)}) async-start(f32[1,512,256]{2,0,1:T(1,128)} %copy.245), calls=%async_computation | async-start | bytes 1048576 | tf_op jit(solution)/shard_map/all_to_all | solution.py:213
  77.9 0.8 copy-start.7
  78.7 34.9 %all-to-all-start.11 = ((f32[128,8,256]{2,1,0:T(8,128)}), f32[128,8,256]{2,1,0:T(8,128)S(1)}, u32[]{:S(2)}, u32[]{:S(2)}) async-start(f32[128,8,256]{2,1,0:T(8,128)} %copy.295), calls=%async_computation.11 | async-start | bytes 2097152 | tf_op jit(solution)/shard_map/all_to_all | solution.py:163
  85.5 33.7 %copy-start.10 = (bf16[64,2,1024]{2,1,0:T(2,128)(2,1)S(1)}, bf16[64,2,1024]{2,1,0:T(2,128)(2,1)}, u32[]{:S(2)}) copy-start(bf16[64,2,1024]{2,1,0:T(2,128)(2,1)} %copy-done.9) | copy-start | bytes 786436
  113.6 34.5 %all-to-all-start.10 = ((f32[128,8,256]{2,1,0:T(8,128)}), f32[128,8,256]{2,1,0:T(8,128)S(1)}, u32[]{:S(2)}, u32[]{:S(2)}) async-start(f32[128,8,256]{2,1,0:T(8,128)} %copy.292), calls=%async_computation.10 | async-start | bytes 2097152 | tf_op jit(solution)/shard_map/all_to_all | solution.py:162
  148.1 8.2 copy-start.6
  148.1 34.6 %all-to-all-start.5 = ((f32[128,8,256]{2,1,0:T(8,128)}), f32[128,8,256]{2,1,0:T(8,128)}, u32[]{:S(2)}, u32[]{:S(2)}) async-start(f32[128,8,256]{2,1,0:T(8,128)} %copy.265), calls=%async_computation.5 | async-start | bytes 2097152 | tf_op jit(solution)/shard_map/all_to_all | solution.py:163
  182.6 6.0 copy-start.8
  182.6 34.7 %all-to-all-start.4 = ((f32[128,8,256]{2,1,0:T(8,128)}), f32[128,8,256]{2,1,0:T(8,128)}, u32[]{:S(2)}, u32[]{:S(2)}) async-start(f32[128,8,256]{2,1,0:T(8,128)} %copy.262), calls=%async_computation.4 | async-start | bytes 2097152 | tf_op jit(solution)/shard_map/all_to_all | solution.py:162
  217.3 34.6 %all-to-all-start.2 = ((f32[128,8,256]{2,1,0:T(8,128)}), f32[128,8,256]{2,1,0:T(8,128)}, u32[]{:S(2)}, u32[]{:S(2)}) async-start(f32[128,8,256]{2,1,0:T(8,128)} %copy.250), calls=%async_computation.2 | async-start | bytes 2097152 | tf_op jit(solution)/shard_map/all_to_all | solution.py:163
  251.9 34.6 %all-to-all-start.1 = ((f32[128,8,256]{2,1,0:T(8,128)}), f32[128,8,256]{2,1,0:T(8,128)}, u32[]{:S(2)}, u32[]{:S(2)}) async-start(f32[128,8,256]{2,1,0:T(8,128)} %copy.247), calls=%async_computation.1 | async-start | bytes 2097152 | tf_op jit(solution)/shard_map/all_to_all | solution.py:162
  286.5 1.5 copy-start.4
  286.5 1.9 copy-start.5
  356.0 34.6 %all-to-all-start.6 = ((f32[2,512,256]{2,0,1:T(2,128)}), f32[2,512,256]{2,0,1:T(2,128)}, u32[]{:S(2)}, u32[]{:S(2)}) async-start(f32[2,512,256]{2,0,1:T(2,128)} %copy.283), calls=%async_computation.6 | async-start | bytes 2097152 | tf_op jit(solution)/shard_map/all_to_all | solution.py:185
  361.8 4.1 copy-start.1
  390.5 59.7 %all-to-all-start.12 = ((f32[2,512,512]{2,0,1:T(2,128)}), f32[2,512,512]{2,0,1:T(2,128)}, u32[]{:S(2)}, u32[]{:S(2)}) async-start(f32[2,512,512]{2,0,1:T(2,128)} %copy.311), calls=%async_computation.12 | async-start | bytes 4194304 | tf_op jit(solution)/shard_map/all_to_all | solution.py:185
  450.3 56.7 %all-to-all-start.13 = ((f32[2,512,512]{2,0,1:T(2,128)}), f32[2,512,512]{2,0,1:T(2,128)S(1)}, u32[]{:S(2)}, u32[]{:S(2)}) async-start(f32[2,512,512]{2,0,1:T(2,128)} %copy.314), calls=%async_computation.13 | async-start | bytes 4194304 | tf_op jit(solution)/shard_map/all_to_all | solution.py:186
  507.0 34.3 %all-to-all-start.7 = ((f32[2,512,256]{2,0,1:T(2,128)}), f32[2,512,256]{2,0,1:T(2,128)}, u32[]{:S(2)}, u32[]{:S(2)}) async-start(f32[2,512,256]{2,0,1:T(2,128)} %copy.286), calls=%async_computation.7 | async-start | bytes 2097152 | tf_op jit(solution)/shard_map/all_to_all | solution.py:186
  524.6 3.8 copy-start.2
  528.4 1.6 copy-start.3
  541.3 34.8 %all-to-all-start.14 = ((f32[64,8,512]{2,1,0:T(8,128)}), f32[64,8,512]{2,1,0:T(8,128)}, u32[]{:S(2)}, u32[]{:S(2)}) async-start(f32[64,8,512]{2,1,0:T(8,128)} %copy.317), calls=%async_computation.14 | async-start | bytes 2097152 | tf_op jit(solution)/shard_map/all_to_all | solution.py:189
  556.8 24.9 %copy-start.20 = (f32[256]{0:T(256)S(1)}, f32[256]{0:T(256)}, u32[]{:S(2)}) copy-start(f32[256]{0:T(256)} %copy-done.19) | copy-start | bytes 3076
  556.9 42.4 %copy-start.11 = (bf16[512,256]{1,0:T(8,128)(2,1)S(1)}, bf16[512,256]{1,0:T(8,128)(2,1)}, u32[]{:S(2)}) copy-start(bf16[512,256]{1,0:T(8,128)(2,1)} %param.10) | copy-start | bytes 786436
  556.9 42.4 %copy-start.12 = (bf16[512,256]{1,0:T(8,128)(2,1)S(1)}, bf16[512,256]{1,0:T(8,128)(2,1)}, u32[]{:S(2)}) copy-start(bf16[512,256]{1,0:T(8,128)(2,1)} %param.11) | copy-start | bytes 786436
  556.9 42.4 %copy-start.14 = (bf16[512,256]{1,0:T(8,128)(2,1)S(1)}, bf16[512,256]{1,0:T(8,128)(2,1)}, u32[]{:S(2)}) copy-start(bf16[512,256]{1,0:T(8,128)(2,1)} %param.9) | copy-start | bytes 786436
  556.9 42.4 %copy-start.21 = (f32[256]{0:T(256)S(1)}, f32[256]{0:T(256)}, u32[]{:S(2)}) copy-start(f32[256]{0:T(256)} %get-tuple-element.63) | copy-start | bytes 3076
  556.9 42.4 %copy-start.23 = (f32[256]{0:T(256)S(1)}, f32[256]{0:T(256)}, u32[]{:S(2)}) copy-start(f32[256]{0:T(256)} %param.12) | copy-start | bytes 3076
  576.1 23.2 %all-to-all-start.8 = ((f32[64,8,256]{2,1,0:T(8,128)}), f32[64,8,256]{2,1,0:T(8,128)S(1)}, u32[]{:S(2)}, u32[]{:S(2)}) async-start(f32[64,8,256]{2,1,0:T(8,128)} %copy.289), calls=%async_computation.8 | async-start | bytes 1048576 | tf_op jit(solution)/shard_map/all_to_all | solution.py:189
  581.6 173.6 %all-reduce.4.cloned.1.call-start = ((), (), s32[]{:S(2)}) async-start(), calls=%async_computation.15 | async-start | bytes 131072 | tf_op jit(solution)/shard_map/psum | solution.py:260
  584.4 215.8 %all-reduce.6.cloned.1.call-start = ((), (), s32[]{:S(2)}) async-start(), calls=%async_computation.16 | async-start | bytes 262144 | tf_op jit(solution)/shard_map/psum | solution.py:258
  586.9 213.2 %copy-start.16 = (f32[64,64]{1,0:T(8,128)S(1)}, f32[64,64]{1,0:T(8,128)}, u32[]{:S(2)}) copy-start(f32[64,64]{1,0:T(8,128)} %param.16) | copy-start | bytes 49156
Sparse Core Ops, SparseCore 0:
  586.5 168.6 all-reduce.3
  757.5 42.5 all-reduce.5
where the time goes:
time: 1080 us; the launch traced here: 1070 us
  waiting for transfers between devices  508 us (47%)
  blocking collectives  249 us (23%)
  starting transfers between devices  103 us (10%)
  matrix products  102 us (9%)
  local copies, waits for them, and re-layouts  69 us (6%)
  other arithmetic  19.3 us (2%)
  between operations  15.4 us (1%)
    psum x1, blocking collectives, on_device(): lax.psum((out_part, skip_part, rate_part, embed_part, mid_part, freq_part...  249 us
    psum x1, waiting for transfers between devices, on_device(): lax.psum((out_part, skip_part, rate_part, embed_part, mid_part, freq_part...  153 us
    dot_general x50, matrix products, einsum_high(): return jnp.einsum(pattern, matrix, values, precision=highest)  90.5 us
    all_to_all x3, waiting for transfers between devices, to_spectrum(): lax.all_to_all(columns[1], 'seq', split_axis=0, concat_axis=1, tiled=True)  78.8 us
    all_to_all x3, waiting for transfers between devices, to_spectrum(): lax.all_to_all(columns[0], 'seq', split_axis=0, concat_axis=1, tiled=True)  61.6 us
    all_to_all x2, waiting for transfers between devices, to_positions(): lax.all_to_all(packed[1], 'seq', split_axis=1, concat_axis=0, tiled=True)  56.7 us
    all_to_all x2, waiting for transfers between devices, to_positions(): lax.all_to_all(packed[0], 'seq', split_axis=1, concat_axis=0, tiled=True)  50.3 us
    psum x1, waiting for transfers between devices, on_device(): upper_grad = lax.psum(upper_grad, 'ch')  43.4 us
  transfers between devices with their start and end apart: 17, of which 17 were waited for; matrix products, arithmetic and copies ran while one was open for 9% of the time, Pallas kernels for 0%

commit v1 on v0

--- a/solution.py
+++ b/solution.py
@@ -255,7 +255,7 @@
     upper_grad = jnp.dot(
         scaled_kernel, out_weight.T, precision=highest, preferred_element_type=jnp.float32
     )
-    upper_grad = lax.psum(upper_grad, "ch")
+    upper_grad = jnp.sum(lax.all_gather(upper_grad, "ch"), axis=0)
     embed_part, freq_part, mid_part = lower_pull(upper_grad)
     out_sum, skip_sum, rate_sum, embed_sum, mid_sum, freq_sum = lax.psum(
         (out_part, skip_part, rate_part, embed_part, mid_part, freq_part), "seq"

time: 1080 us -> 1040 us (0.963)
  waiting for transfers between devices: 508 us -> 463 us
  blocking collectives: 249 us -> 261 us
    psum x1 -> x0, waiting for transfers between devices: 43.4 us -> none  [on_device(): upper_grad = lax.psum(upper_grad, 'ch')]
    all_to_all x2, waiting for transfers between devices: 30.4 us -> 18.1 us  [to_positions(): lax.all_to_all(rows_back, 'seq', split_axis=0, concat_axis=1, tiled=True)]
    all_gather x0 -> x1, blocking collectives: none -> 11.8 us  [on_device(): upper_grad = jnp.sum(lax.all_gather(upper_grad, 'ch'), axis=0)]
    psum x1, waiting for transfers between devices: 153 us -> 164 us  [on_device(): lax.psum((out_part, skip_part, rate_part, embed_part, mid_part, freq_part...]
  transfers between devices with their start and end apart: 17 -> 16, of which waited for: 17 -> 15; matrix products, arithmetic and copies ran while one was open for 9% -> 9% of each run, Pallas kernels for 0% -> 0%
where the time goes in v1:
time: 1040 us; the launch traced here: 1030 us
  waiting for transfers between devices  463 us (45%)
  blocking collectives  261 us (25%)
  starting transfers between devices  103 us (10%)
  matrix products  101 us (10%)
  local copies, waits for them, and re-layouts  69.3 us (7%)
  other arithmetic  18.7 us (2%)
  between operations  15.5 us (1%)
    psum x1, blocking collectives, on_device(): lax.psum((out_part, skip_part, rate_part, embed_part, mid_part, freq_part...  249 us
    psum x1, waiting for transfers between devices, on_device(): lax.psum((out_part, skip_part, rate_part, embed_part, mid_part, freq_part...  164 us
    dot_general x50, matrix products, einsum_high(): return jnp.einsum(pattern, matrix, values, precision=highest)  90.5 us
    all_to_all x3, waiting for transfers between devices, to_spectrum(): lax.all_to_all(columns[1], 'seq', split_axis=0, concat_axis=1, tiled=True)  78.8 us
    all_to_all x3, waiting for transfers between devices, to_spectrum(): lax.all_to_all(columns[0], 'seq', split_axis=0, concat_axis=1, tiled=True)  61.6 us
    all_to_all x2, waiting for transfers between devices, to_positions(): lax.all_to_all(packed[1], 'seq', split_axis=1, concat_axis=0, tiled=True)  56.8 us
    all_to_all x2, waiting for transfers between devices, to_positions(): lax.all_to_all(packed[0], 'seq', split_axis=1, concat_axis=0, tiled=True)  50.3 us
    all_to_all x3, starting transfers between devices, to_spectrum(): lax.all_to_all(columns[0], 'seq', split_axis=0, concat_axis=1, tiled=True)  26.1 us
  transfers between devices with their start and end apart: 16, of which 15 were waited for; matrix products, arithmetic and copies ran while one was open for 9% of the time, Pallas kernels for 0%

profile of v1, /device:TPU:4, one launch (start us, length us, event | category | flops | bytes accessed | tf_op | source)
XLA Modules:
  0.0 1030.7 jit_solution(14200954759905543499)
XLA Ops:
  9.3 2.2 reduce
  12.3 12.1 %all-to-all-start.9 = ((bf16[64,2,1024]{2,1,0:T(2,128)(2,1)}), bf16[64,2,1024]{2,1,0:T(2,128)(2,1)S(1)}, u32[]{:S(2)}, u32[]{:S(2)}) async-start(bf16[64,2,1024]{2,1,0:T(2,128)(2,1)} %reshape.244), calls=%async_computation.9 | async-start | bytes 524288 | tf_op jit(solution)/shard_map/all_to_all | solution.py:223
  24.9 2.2 reduce.1
  29.3 8.1 all-to-all-done.9
  37.4 4.9 all-to-all-start.3
  45.5 9.8 all-to-all-done.3
  55.3 4.9 all-to-all-start
  62.9 15.0 %all-to-all-done = f32[1,512,256]{2,0,1:T(1,128)S(1)} async-done(((f32[1,512,256]{2,0,1:T(1,128)}), f32[1,512,256]{2,0,1:T(1,128)S(1)}, u32[]{:S(2)}, u32[]{:S(2)}) %all-to-all-start) | async-done | bytes 524320 | tf_op jit(solution)/shard_map/all_to_all | solution.py:213
  78.7 6.0 all-to-all-start.11
  87.1 26.5 %all-to-all-done.11 = f32[128,8,256]{2,1,0:T(8,128)S(1)} async-done(((f32[128,8,256]{2,1,0:T(8,128)}), f32[128,8,256]{2,1,0:T(8,128)S(1)}, u32[]{:S(2)}, u32[]{:S(2)}) %all-to-all-start.11) | async-done | bytes 1048608 | tf_op jit(solution)/shard_map/all_to_all | solution.py:163
  113.6 5.6 all-to-all-start.10
  123.6 24.5 %all-to-all-done.10 = f32[128,8,256]{2,1,0:T(8,128)S(1)} async-done(((f32[128,8,256]{2,1,0:T(8,128)}), f32[128,8,256]{2,1,0:T(8,128)S(1)}, u32[]{:S(2)}, u32[]{:S(2)}) %all-to-all-start.10) | async-done | bytes 1048608 | tf_op jit(solution)/shard_map/all_to_all | solution.py:162
  148.1 5.8 all-to-all-start.5
  156.2 26.4 %all-to-all-done.5 = f32[128,8,256]{2,1,0:T(8,128)} async-done(((f32[128,8,256]{2,1,0:T(8,128)}), f32[128,8,256]{2,1,0:T(8,128)}, u32[]{:S(2)}, u32[]{:S(2)}) %all-to-all-start.5) | async-done | bytes 1048608 | tf_op jit(solution)/shard_map/all_to_all | solution.py:163
  182.6 6.0 all-to-all-start.4
  191.4 25.9 %all-to-all-done.4 = f32[128,8,256]{2,1,0:T(8,128)} async-done(((f32[128,8,256]{2,1,0:T(8,128)}), f32[128,8,256]{2,1,0:T(8,128)}, u32[]{:S(2)}, u32[]{:S(2)}) %all-to-all-start.4) | async-done | bytes 1048608 | tf_op jit(solution)/shard_map/all_to_all | solution.py:162
  217.3 5.8 all-to-all-start.2
  226.0 25.9 %all-to-all-done.2 = f32[128,8,256]{2,1,0:T(8,128)} async-done(((f32[128,8,256]{2,1,0:T(8,128)}), f32[128,8,256]{2,1,0:T(8,128)}, u32[]{:S(2)}, u32[]{:S(2)}) %all-to-all-start.2) | async-done | bytes 1048608 | tf_op jit(solution)/shard_map/all_to_all | solution.py:163
  251.9 14.6 %all-to-all-start.1 = ((f32[128,8,256]{2,1,0:T(8,128)}), f32[128,8,256]{2,1,0:T(8,128)}, u32[]{:S(2)}, u32[]{:S(2)}) async-start(f32[128,8,256]{2,1,0:T(8,128)} %copy.247), calls=%async_computation.1 | async-start | bytes 2097152 | tf_op jit(solution)/shard_map/all_to_all | solution.py:162
  268.4 2.3 copy.266
  270.7 2.3 copy.263
  273.0 2.3 copy.251
  275.3 11.2 %all-to-all-done.1 = f32[128,8,256]{2,1,0:T(8,128)} async-done(((f32[128,8,256]{2,1,0:T(8,128)}), f32[128,8,256]{2,1,0:T(8,128)}, u32[]{:S(2)}, u32[]{:S(2)}) %all-to-all-start.1) | async-done | bytes 1048608 | tf_op jit(solution)/shard_map/all_to_all | solution.py:162
  288.3 2.1 fusion.28
  308.6 2.4 multiply_subtract_fusion
  312.6 2.1 fusion.60
  325.0 1.9 fusion.72
  330.4 2.4 add_bitcast_fusion.3
  332.8 3.4 fusion.10
  336.2 3.5 fusion.11
  354.0 2.0 copy.283
  356.0 5.8 all-to-all-start.6
  361.8 4.0 fusion.14
  365.9 3.0 subtract_bitcast_fusion.1
  368.8 3.2 fusion.4
  372.0 3.4 subtract_bitcast_fusion
  377.1 3.2 fusion.2
  380.3 3.4 add_bitcast_fusion
  385.5 2.9 copy.311
  388.4 2.1 all-to-all-done.6
  390.5 8.6 all-to-all-start.12
  399.1 3.0 copy.314
  402.1 48.2 %all-to-all-done.12 = f32[2,512,512]{2,0,1:T(2,128)} async-done(((f32[2,512,512]{2,0,1:T(2,128)}), f32[2,512,512]{2,0,1:T(2,128)}, u32[]{:S(2)}, u32[]{:S(2)}) %all-to-all-start.12) | async-done | bytes 2097184 | tf_op jit(solution)/shard_map/all_to_all | solution.py:185
  450.3 5.3 all-to-all-start.13
  455.6 3.0 copy.286
  458.6 48.3 %all-to-all-done.13 = f32[2,512,512]{2,0,1:T(2,128)S(1)} async-done(((f32[2,512,512]{2,0,1:T(2,128)}), f32[2,512,512]{2,0,1:T(2,128)S(1)}, u32[]{:S(2)}, u32[]{:S(2)}) %all-to-all-start.13) | async-done | bytes 2097184 | tf_op jit(solution)/shard_map/all_to_all | solution.py:186
  507.0 5.6 all-to-all-start.7
  512.6 2.0 copy.419
  514.6 2.9 copy.313
  517.5 3.7 all_to_all.213
  521.6 3.0 copy.316
  524.6 3.8 all_to_all.217
  532.9 8.4 all-to-all-done.7
  541.3 6.0 all-to-all-start.14
  553.3 1.9 all_to_all.198
  558.0 18.1 %all-to-all-done.14 = f32[64,8,512]{2,1,0:T(8,128)} async-done(((f32[64,8,512]{2,1,0:T(8,128)}), f32[64,8,512]{2,1,0:T(8,128)}, u32[]{:S(2)}, u32[]{:S(2)}) %all-to-all-start.14) | async-done | bytes 1048608 | tf_op jit(solution)/shard_map/all_to_all | solution.py:189
  576.1 5.6 all-to-all-start.8
  581.7 1.8 fusion.96
  583.6 11.8 %all-gather = f32[2048,64]{0,1:T(8,128)S(1)} all-gather(f32[512,64]{0,1:T(8,128)S(1)} %fusion.96), channel_id=2, replica_groups=mesh['seq'=64,'ch'=4] {'ch'}, dimensions={0}, use_global_device_ids=true | all-gather | bytes 655360 | tf_op jit(solution)/shard_map/all_gather | solution.py:258
  596.7 1.9 multiply_reduce_fusion.1
  600.2 2.6 fusion.98
  602.9 2.5 multiply_reduce_fusion
  605.4 249.2 %all-reduce = (f32[256]{0:T(256)S(1)}, f32[256]{0:T(256)S(1)}, f32[33,64]{1,0:T(8,128)S(1)}, f32[64,64]{1,0:T(8,128)S(1)}, f32[64]{0:T(128)S(1)}) all-reduce(f32[256]{0:T(256)S(1)} %get-tuple-element.48, f32[256]{0:T(256)S(1)} %get-tuple-element.44, f32[33,64]{1,0:T(8,128)S(1)} %fusion.114, ...), channel_id=1, replica_groups=mesh['seq'=64,'ch'=4] {'seq'}, use_global_device_ids=true, to_apply=%region_1.2 | all-reduce | flops 6784 | bytes 54272 | tf_op jit(solution)/shard_map/psum | solution.py:260
  857.5 164.5 %all-reduce.3.cloned.1.call-done = f32[64,256]{1,0:T(8,128)} async-done(((f32[64,256]{1,0:T(8,128)}), f32[64,256]{1,0:T(8,128)}) %all-reduce.3.cloned.1.call-update) | async-done | bytes 65552 | tf_op jit(solution)/shard_map/psum | solution.py:260
  (152 shorter events, 102.2 us)
Async XLA Ops:
  7.2 35.7 %copy-start = (f32[64,256]{1,0:T(8,128)S(1)}, f32[64,256]{1,0:T(8,128)}, u32[]{:S(2)}) copy-start(f32[64,256]{1,0:T(8,128)} %param.17) | copy-start | bytes 196612
  7.2 17.3 %copy-start.13 = (bf16[512,256]{1,0:T(8,128)(2,1)S(1)}, bf16[512,256]{1,0:T(8,128)(2,1)}, u32[]{:S(2)}) copy-start(bf16[512,256]{1,0:T(8,128)(2,1)} %param.9) | copy-start | bytes 786436
  8.8 19.4 %copy-start.17 = (f32[33,64]{1,0:T(8,128)S(1)}, f32[33,64]{1,0:T(8,128)}, u32[]{:S(2)}) copy-start(f32[33,64]{1,0:T(8,128)} %param.14) | copy-start | bytes 25348
  9.3 19.2 %copy-start.15 = (f32[64,64]{1,0:T(8,128)S(1)}, f32[64,64]{1,0:T(8,128)}, u32[]{:S(2)}) copy-start(f32[64,64]{1,0:T(8,128)} %param.16) | copy-start | bytes 49156
  9.3 19.2 %copy-start.16 = (f32[64]{0:T(128)S(1)}, f32[64]{0:T(128)}, u32[]{:S(2)}) copy-start(f32[64]{0:T(128)} %param.15) | copy-start | bytes 772
  11.5 30.8 %copy-start.22 = (f32[256]{0:T(256)S(1)}, f32[256]{0:T(256)}, u32[]{:S(2)}) copy-start(f32[256]{0:T(256)} %param.13) | copy-start | bytes 3076
  12.3 25.1 %all-to-all-start.9 = ((bf16[64,2,1024]{2,1,0:T(2,128)(2,1)}), bf16[64,2,1024]{2,1,0:T(2,128)(2,1)S(1)}, u32[]{:S(2)}, u32[]{:S(2)}) async-start(bf16[64,2,1024]{2,1,0:T(2,128)(2,1)} %reshape.244), calls=%async_computation.9 | async-start | bytes 524288 | tf_op jit(solution)/shard_map/all_to_all | solution.py:223
  37.4 17.9 %all-to-all-start.3 = ((bf16[64,2,1024]{2,1,0:T(2,128)(2,1)}), bf16[64,2,1024]{2,1,0:T(2,128)(2,1)S(1)}, u32[]{:S(2)}, u32[]{:S(2)}) async-start(bf16[64,2,1024]{2,1,0:T(2,128)(2,1)} %reshape.242), calls=%async_computation.3 | async-start | bytes 524288 | tf_op jit(solution)/shard_map/all_to_all | solution.py:209
  42.9 12.4 %copy-start.18 = (f32[256]{0:T(256)}, f32[256]{0:T(256)S(1)}, u32[]{:S(2)}) copy-start(f32[256]{0:T(256)S(1)} %get-tuple-element.65) | copy-start | bytes 3076
  55.3 5.2 copy-start.9
  55.3 22.6 %all-to-all-start = ((f32[1,512,256]{2,0,1:T(1,128)}), f32[1,512,256]{2,0,1:T(1,128)S(1)}, u32[]{:S(2)}, u32[]{:S(2)}) async-start(f32[1,512,256]{2,0,1:T(1,128)} %copy.245), calls=%async_computation | async-start | bytes 1048576 | tf_op jit(solution)/shard_map/all_to_all | solution.py:213
  77.9 0.8 copy-start.7
  78.7 34.9 %all-to-all-start.11 = ((f32[128,8,256]{2,1,0:T(8,128)}), f32[128,8,256]{2,1,0:T(8,128)S(1)}, u32[]{:S(2)}, u32[]{:S(2)}) async-start(f32[128,8,256]{2,1,0:T(8,128)} %copy.295), calls=%async_computation.11 | async-start | bytes 2097152 | tf_op jit(solution)/shard_map/all_to_all | solution.py:163
  85.5 33.7 %copy-start.10 = (bf16[64,2,1024]{2,1,0:T(2,128)(2,1)S(1)}, bf16[64,2,1024]{2,1,0:T(2,128)(2,1)}, u32[]{:S(2)}) copy-start(bf16[64,2,1024]{2,1,0:T(2,128)(2,1)} %copy-done.9) | copy-start | bytes 786436
  113.6 34.5 %all-to-all-start.10 = ((f32[128,8,256]{2,1,0:T(8,128)}), f32[128,8,256]{2,1,0:T(8,128)S(1)}, u32[]{:S(2)}, u32[]{:S(2)}) async-start(f32[128,8,256]{2,1,0:T(8,128)} %copy.292), calls=%async_computation.10 | async-start | bytes 2097152 | tf_op jit(solution)/shard_map/all_to_all | solution.py:162
  148.1 8.2 copy-start.6
  148.1 34.6 %all-to-all-start.5 = ((f32[128,8,256]{2,1,0:T(8,128)}), f32[128,8,256]{2,1,0:T(8,128)}, u32[]{:S(2)}, u32[]{:S(2)}) async-start(f32[128,8,256]{2,1,0:T(8,128)} %copy.265), calls=%async_computation.5 | async-start | bytes 2097152 | tf_op jit(solution)/shard_map/all_to_all | solution.py:163
  182.6 6.0 copy-start.8
  182.6 34.7 %all-to-all-start.4 = ((f32[128,8,256]{2,1,0:T(8,128)}), f32[128,8,256]{2,1,0:T(8,128)}, u32[]{:S(2)}, u32[]{:S(2)}) async-start(f32[128,8,256]{2,1,0:T(8,128)} %copy.262), calls=%async_computation.4 | async-start | bytes 2097152 | tf_op jit(solution)/shard_map/all_to_all | solution.py:162
  217.3 34.6 %all-to-all-start.2 = ((f32[128,8,256]{2,1,0:T(8,128)}), f32[128,8,256]{2,1,0:T(8,128)}, u32[]{:S(2)}, u32[]{:S(2)}) async-start(f32[128,8,256]{2,1,0:T(8,128)} %copy.250), calls=%async_computation.2 | async-start | bytes 2097152 | tf_op jit(solution)/shard_map/all_to_all | solution.py:163
  251.9 34.6 %all-to-all-start.1 = ((f32[128,8,256]{2,1,0:T(8,128)}), f32[128,8,256]{2,1,0:T(8,128)}, u32[]{:S(2)}, u32[]{:S(2)}) async-start(f32[128,8,256]{2,1,0:T(8,128)} %copy.247), calls=%async_computation.1 | async-start | bytes 2097152 | tf_op jit(solution)/shard_map/all_to_all | solution.py:162
  286.4 1.5 copy-start.4
  286.4 1.9 copy-start.5
  356.0 34.6 %all-to-all-start.6 = ((f32[2,512,256]{2,0,1:T(2,128)}), f32[2,512,256]{2,0,1:T(2,128)}, u32[]{:S(2)}, u32[]{:S(2)}) async-start(f32[2,512,256]{2,0,1:T(2,128)} %copy.283), calls=%async_computation.6 | async-start | bytes 2097152 | tf_op jit(solution)/shard_map/all_to_all | solution.py:185
  361.8 4.1 copy-start.1
  390.5 59.7 %all-to-all-start.12 = ((f32[2,512,512]{2,0,1:T(2,128)}), f32[2,512,512]{2,0,1:T(2,128)}, u32[]{:S(2)}, u32[]{:S(2)}) async-start(f32[2,512,512]{2,0,1:T(2,128)} %copy.311), calls=%async_computation.12 | async-start | bytes 4194304 | tf_op jit(solution)/shard_map/all_to_all | solution.py:185
  450.3 56.7 %all-to-all-start.13 = ((f32[2,512,512]{2,0,1:T(2,128)}), f32[2,512,512]{2,0,1:T(2,128)S(1)}, u32[]{:S(2)}, u32[]{:S(2)}) async-start(f32[2,512,512]{2,0,1:T(2,128)} %copy.314), calls=%async_computation.13 | async-start | bytes 4194304 | tf_op jit(solution)/shard_map/all_to_all | solution.py:186
  507.0 34.3 %all-to-all-start.7 = ((f32[2,512,256]{2,0,1:T(2,128)}), f32[2,512,256]{2,0,1:T(2,128)}, u32[]{:S(2)}, u32[]{:S(2)}) async-start(f32[2,512,256]{2,0,1:T(2,128)} %copy.286), calls=%async_computation.7 | async-start | bytes 2097152 | tf_op jit(solution)/shard_map/all_to_all | solution.py:186
  524.6 3.8 copy-start.2
  528.4 1.6 copy-start.3
  541.3 34.8 %all-to-all-start.14 = ((f32[64,8,512]{2,1,0:T(8,128)}), f32[64,8,512]{2,1,0:T(8,128)}, u32[]{:S(2)}, u32[]{:S(2)}) async-start(f32[64,8,512]{2,1,0:T(8,128)} %copy.317), calls=%async_computation.14 | async-start | bytes 2097152 | tf_op jit(solution)/shard_map/all_to_all | solution.py:189
  556.1 25.7 %copy-start.19 = (f32[256]{0:T(256)S(1)}, f32[256]{0:T(256)}, u32[]{:S(2)}) copy-start(f32[256]{0:T(256)} %copy-done.18) | copy-start | bytes 3076
  576.1 26.8 %all-to-all-start.8 = ((f32[64,8,256]{2,1,0:T(8,128)}), f32[64,8,256]{2,1,0:T(8,128)S(1)}, u32[]{:S(2)}, u32[]{:S(2)}) async-start(f32[64,8,256]{2,1,0:T(8,128)} %copy.289), calls=%async_computation.8 | async-start | bytes 1048576 | tf_op jit(solution)/shard_map/all_to_all | solution.py:189
  581.7 440.3 %all-reduce.3.cloned.1.call-start = ((), (), s32[]{:S(2)}) async-start(), calls=%async_computation.15 | async-start | bytes 131072 | tf_op jit(solution)/shard_map/psum | solution.py:260
  595.4 7.5 copy-start.11
  595.4 7.5 copy-start.12
  595.7 7.1 copy-start.14
  595.7 7.1 copy-start.20
  595.8 7.1 copy-start.21
  595.8 7.1 copy-start.23
Sparse Core Ops, SparseCore 0:
  857.1 164.8 all-reduce.2
